TPU v7x, 32 devices: a whole 2x2x4 slice. The times are simulated.
32 devices in a mesh: sens: 4 (over y, x), par: 8 (over z, core).
Axes of the slice: x: 2, y: 2, z: 4, core: 2. Of those that a mesh axis runs over, the one named last changes fastest.
Arguments:
- kernel: bfloat16 [2, 129, 64, 8192], P(None, None, 'sens', 'par'), may hold values from -0.0625 to 0.0625
- param: float32 [128, 2, 8192], P(None, None, 'par'), may hold values from -6 to 6
- observed: float32 [64, 128], P('sens'), may hold values from -6 to 6
- noise_scale: float32 [64], P('sens'), may hold values from 0.3 to 3
- robust_flags: int32 [64, 128], P('sens'), may hold values 0 or 1
- kappa_field: float32 [8192], P('par'), may hold values from 0.01 to 0.1
- coupling: float32 [8192], P('par'), may hold values from 0.05 to 0.2
- neighbours: int32 [8, 4], replicated, may hold values from -1 to 7, as said below
Outputs:
- gradient: float32 [128, 2, 8192], P(None, None, 'par')
- direction: float32 [128, 2, 8192], P(None, None, 'par')
Inputs may be any that keep to these rules, and one draw needn't show every extreme that they name: `neighbours`: row k lists the tiles west, east, south and north of tile k, or -1 where there is none; the tiles fill a grid of 2 columns and 4 rows in an order drawn from the seed, and the relations are mutual.
All inputs are finite; a program needn't handle non-finite values. No bound on the sum of `robust_flags` on one device may be relied on, other than what follows from the above.
Results may differ from a plain program's by a relative error of at most 0.003.
Values may be sent and summed in bfloat16 or wider, within the bound.
A program may use at most 128 MiB of HBM per device.

v0:
```python
import functools

import jax
import jax.numpy as jnp
import numpy as np
from jax import lax
from jax.experimental import pallas as pl
from jax.experimental.pallas import tpu as pltpu
from jax.sharding import PartitionSpec as P

SWEEPS = 8
TSIDE = 32
LANES = 128
GROUP = 16
HALF = 8
WIDE = 256

huber_limit = 1.345

MESH = pl.DeviceIdType.MESH
LAST = (((1,), (1,)), ((), ()))
f32, bf16 = jnp.float32, jnp.bfloat16


def tables(length):
    period = 2 * length
    frequency = np.arange(length + 1)
    phases = frequency[:, None] * np.arange(length)[None, :] % period
    angles = phases * (2.0 * np.pi / period)
    cosine, sines = np.cos(angles), np.sin(angles)
    forward = np.stack([cosine, -sines], 0)
    weight = np.where((frequency == 0) | (frequency == length), 1.0, 2.0) / period
    return forward, forward * weight[:, None]


def halves(table):
    high = table.astype(np.float32).astype(jnp.bfloat16)
    low = (table - high.astype(np.float64)).astype(np.float32).astype(jnp.bfloat16)
    return high, low


def pairs(table):
    high, low = halves(table)
    return np.concatenate(
        [np.concatenate([high, high], 1), np.concatenate([low, np.zeros_like(low)], 1)], 0
    )


def all_tables(length):
    forward, backward = tables(length)
    count = length + 1
    groups = -(-count // GROUP)
    full = count // GROUP
    pad = ((0, 0), (0, groups * GROUP - count), (0, 0))

    def rows(table):
        table = np.pad(table, pad).reshape(2, groups, GROUP, length)
        return table.transpose(1, 0, 2, 3).reshape(groups * 2 * GROUP, length)

    fore, back = rows(forward), rows(backward)
    trans = np.pad(backward, pad).reshape(2, groups, 2, HALF, length)
    trans = trans.transpose(0, 2, 4, 1, 3).reshape(4 * length, groups * HALF)
    high, low = (part.T for part in halves(fore))
    cut = full * 2 * GROUP
    main, rest = slice(0, cut), slice(cut, None)
    misfit = np.concatenate(
        [high[:, main], high[:, main], low[:, main], high[:, rest], high[:, rest], low[:, rest]], 1
    )
    return pairs(fore), pairs(trans), pairs(back), misfit


def split(values):
    high = values.astype(bf16)
    return high, (values - high.astype(f32)).astype(bf16)


def split_wide(values):
    high = values.astype(bf16).astype(f32)
    return high, values - high


def remote(src, dst, send, recv, device):
    return pltpu.make_async_remote_copy(
        src_ref=src, dst_ref=dst, send_sem=send, recv_sem=recv, device_id=device, device_id_type=MESH
    )


def around(own, chunks, west, east, south, north):
    shape = own[0].shape
    lane = lax.broadcasted_iota(jnp.int32, shape, 1)
    column = lax.rem(lane, TSIDE)
    up = [pltpu.roll(v, LANES - TSIDE, 1) for v in own] + [north]
    down = [south] + [pltpu.roll(v, TSIDE, 1) for v in own]
    sums = []
    for j in range(chunks):
        east_side = jnp.where(column == TSIDE - 1, east(j), pltpu.roll(own[j], LANES - 1, 1))
        west_side = jnp.where(column == 0, west(j), pltpu.roll(own[j], 1, 1))
        north_side = jnp.where(lane < LANES - TSIDE, up[j], up[j + 1])
        south_side = jnp.where(lane >= TSIDE, down[j + 1], down[j])
        sums.append((east_side + west_side) + (north_side + south_side))
    return sums


def main_kernel(
    groups, tiles,
    kernel, param, observed, noise, flags, kappa, coupling, near, fore, trans, back, mist,
    grad_out, dir_out,
    blocks, halved, spectrum, packed, seen, bounded, wide, stacked, misfit, parts, landed, prior,
    rim, rims, kappas, couplings, grad, exact, grad_in, start, ratio, even, odd, dir_send, grad_all, dir_all,
    predicted, k_sem, k_send, k_recv, r_send, r_recv, c_send, c_recv, a_send, a_recv, e_send, e_recv,
    b_send, b_recv, d_send, d_recv, f_send, f_recv,
):
    sens, par = lax.axis_index("sens"), lax.axis_index("par")
    sensors, length = observed.shape
    freqs, pieces = spectrum.shape[0], blocks.shape[1]
    cells = halved.shape[2]
    samples = halved.shape[0]
    full = (length + 1) // GROUP
    chunks = cells // LANES
    columns = cells // WIDE
    stride = chunks * samples
    span = prior.shape[1]
    rows = span // tiles
    group_at = [lax.rem(sens + k, groups) for k in range(groups)]
    tile_at = [lax.rem(par + q, tiles) for q in range(tiles)]
    source_at = [lax.rem(par + tiles - q, tiles) for q in range(tiles)]

    barrier = pltpu.get_barrier_semaphore()
    for k in range(1, groups):
        pl.semaphore_signal(barrier, inc=1, device_id=(group_at[k], par), device_id_type=MESH)
    for q in range(1, tiles):
        pl.semaphore_signal(barrier, inc=1, device_id=(sens, tile_at[q]), device_id_type=MESH)

    loads = []
    for g in range(freqs):
        size = GROUP * sensors if g < full else (length + 1 - full * GROUP) * sensors
        for i in range(pieces):
            copy = pltpu.make_async_copy(
                kernel.at[i, pl.ds(g * GROUP * sensors, size)],
                blocks.at[g, i, pl.ds(0, size)],
                k_sem.at[g, i],
            )
            copy.start()
            loads.append(copy)

    for b in range(samples):
        for j in range(chunks):
            high, low = split(param[pl.ds(samples * j + b, length, stride=stride), :])
            at = slice(j * LANES, (j + 1) * LANES)
            halved[b, :length, at] = high
            halved[b, length:, at] = low

    half = freqs * 2 * GROUP
    for b in range(samples):
        for n in range(columns):
            at = slice(n * WIDE, (n + 1) * WIDE)
            both = jnp.dot(fore[...], halved[b, :, at], preferred_element_type=f32)
            rounded = (both[:half] + both[half:]).astype(bf16)
            for g in range(freqs):
                for k in range(2):
                    to, fro = (k * samples + b) * GROUP, (g * 2 + k) * GROUP
                    spectrum[g, to : to + GROUP, at] = rounded[fro : fro + GROUP]

    copies = LANES // sensors
    seen[...] = jnp.concatenate([observed[...]] * copies, 0).T
    bounded[...] = jnp.concatenate([flags[...].astype(f32)] * copies, 0).T
    deviation = jnp.concatenate([noise[...]] * copies, 1)
    inverse = 1.0 / deviation

    lanes64 = lax.broadcasted_iota(jnp.int32, (2 * samples * GROUP, WIDE), 1) // sensors
    rows64 = lax.rem(lax.broadcasted_iota(jnp.int32, (2 * samples * GROUP, WIDE), 0), GROUP)
    keep = lanes64 == rows64
    place = lax.broadcasted_iota(jnp.int32, (HALF, LANES), 1) // sensors
    side = samples * GROUP

    def pack(real, imag):
        total = jnp.concatenate([real[:side] - imag[side:], real[side:] + imag[:side]], 0)
        for step in range(copies.bit_length() - 1):
            total = total + pltpu.roll(total, sensors << step, 1)
        out = jnp.zeros((HALF, LANES), f32)
        for r in range(copies):
            out = jnp.where(place == r, total[r * HALF : (r + 1) * HALF], out)
        return out

    p_copies = []
    for g in range(freqs):
        for i in range(pieces):
            loads[g * pieces + i].wait()
        folded = []
        for i in range(pieces):
            if g < full:
                product = lax.dot_general(
                    spectrum[g], blocks[g, i], LAST, preferred_element_type=f32
                )
                product = jnp.where(keep, product, 0.0)
                folded.append(product[:, :LANES] + product[:, LANES:])
            else:
                product = lax.dot_general(
                    spectrum[g], blocks[g, i, :sensors], LAST, preferred_element_type=f32
                )
                filler = jnp.zeros((product.shape[0], LANES - sensors), f32)
                folded.append(jnp.concatenate([product, filler], 1))
        packed[g] = pack(*folded)
        if g == 0:
            pl.semaphore_wait(barrier, groups + tiles - 2)
        for q in range(1, tiles):
            copy = remote(
                packed.at[g], predicted.at[q - 1, g], k_send.at[g, q - 1], k_recv.at[g, q - 1],
                (sens, tile_at[q]),
            )
            copy.start()
            p_copies.append(copy)

    first = sens * span
    own_sample, own_time = first // length, lax.rem(first, length)
    own = [
        param[pl.ds(own_time * stride + samples * j + own_sample, span, stride=stride), :]
        for j in range(chunks)
    ]
    lane = lax.broadcasted_iota(jnp.int32, (span, LANES), 1)
    column = lax.rem(lane, TSIDE)
    quarter = lane // TSIDE
    edge = jnp.zeros((span, LANES), f32)
    for j in range(chunks):
        edge = jnp.where(column == j, pltpu.roll(own[j], j, 1) if j else own[j], edge)
        shift = (chunks + j - (TSIDE - 1)) % LANES
        edge = jnp.where(column == chunks + j, pltpu.roll(own[j], shift, 1), edge)
    upper = column >= TSIDE // 2
    edge = jnp.where(upper & (quarter == 0), pltpu.roll(own[0], 16, 1), edge)
    edge = jnp.where(upper & (quarter == 1), pltpu.roll(own[0], 32, 1), edge)
    edge = jnp.where(upper & (quarter == 2), pltpu.roll(own[-1], LANES - 16, 1), edge)
    edge = jnp.where(upper & (quarter == 3), own[-1], edge)
    rim[...] = edge.astype(bf16)
    c_copies = []
    for q in range(1, tiles):
        device = (sens, tile_at[q])
        c_copies.append(remote(rim, rims.at[par], r_send.at[q - 1], r_recv.at[q - 1], device))
        c_copies.append(
            remote(kappa, kappas.at[par], c_send.at[0, q - 1], c_recv.at[0, q - 1], device)
        )
        c_copies.append(
            remote(coupling, couplings.at[par], c_send.at[1, q - 1], c_recv.at[1, q - 1], device)
        )
    for copy in c_copies:
        copy.start()
    rims[tiles] = jnp.zeros((span, LANES), bf16)
    kappas[par] = kappa[...]
    couplings[par] = coupling[...]

    def beside(tile):
        return [jnp.where(near[s, tile] < 0, tiles, near[s, tile]) for s in range(4)]

    for copy in p_copies:
        copy.wait_recv()
    total = packed[...]
    for q in range(tiles - 1):
        total = total + predicted[q]
    high, low = split_wide(total.reshape(freqs * HALF, LANES))
    right = jnp.concatenate([high, low], 0).astype(bf16)
    both = jnp.dot(trans[...], right, preferred_element_type=f32)
    both = both[: 4 * length] + both[4 * length :]
    where = lax.broadcasted_iota(jnp.int32, (length, LANES), 1) // sensors
    sample_of, kind = lax.rem(where // 2, samples), where // (2 * samples) * 2 + lax.rem(where, 2)
    series = both[:length]
    for part in range(1, 4):
        series = jnp.where(kind == part, both[part * length : (part + 1) * length], series)
    adjoint = []
    for b in range(samples):
        mine = jnp.where(sample_of == b, series, 0.0)
        for step in range(copies.bit_length() - 1):
            mine = mine + pltpu.roll(mine, sensors << step, 1)
        scaled = (mine - seen[...]) * inverse
        robust = jnp.where(bounded[...] == 1.0, jnp.clip(scaled, -huber_limit, huber_limit), scaled)
        high, low = split(robust * inverse)
        both = jnp.dot(back[...], jnp.concatenate([high, low], 0), preferred_element_type=f32)
        adjoint.append(both[:half] + both[half:])
    own_row = lax.broadcasted_iota(jnp.int32, (HALF, LANES), 0)
    blank = jnp.zeros((HALF, LANES), f32)
    for g in range(freqs):
        for k in range(2):
            for b in range(samples):
                fro = (g * 2 + k) * GROUP
                piece = adjoint[b][fro : fro + GROUP]
                pick = [
                    jnp.where(own_row == place, piece[h * HALF : (h + 1) * HALF], 0.0)
                    for h in range(2)
                ]
                here = [
                    jnp.concatenate([pick[0], blank], 0), jnp.concatenate([blank, pick[1]], 0)
                ]
                to = (k * samples + b) * GROUP
                other = ((1 - k) * samples + b) * GROUP
                for h in range(2):
                    at = slice(h * LANES, (h + 1) * LANES)
                    wide[g, to : to + GROUP, at] = here[h].astype(bf16)
                    at = slice(WIDE + h * LANES, WIDE + (h + 1) * LANES)
                    turned = here[h] if k else -here[h]
                    wide[g, other : other + GROUP, at] = turned.astype(bf16)

    deep = full * 2 * GROUP
    a_copies = []
    for n in range(columns):
        at = slice(n * WIDE, (n + 1) * WIDE)
        for g in range(freqs):
            if g < full:
                product = jnp.dot(
                    wide[g], blocks[g, :, :, at].reshape(2 * WIDE, WIDE), preferred_element_type=f32
                )
            else:
                product = jnp.dot(
                    wide[g, :, :sensors], blocks[g, 0, :sensors, at], preferred_element_type=f32
                ) + jnp.dot(
                    wide[g, :, WIDE : WIDE + sensors], blocks[g, 1, :sensors, at],
                    preferred_element_type=f32,
                )
            high, low = split(product)
            for k in range(2):
                for b in range(samples):
                    fro = (k * samples + b) * GROUP
                    if g < full:
                        base, gap = (g * 2 + k) * GROUP, deep
                    else:
                        base, gap = 3 * deep + k * GROUP, 2 * GROUP
                    stacked[b, base : base + GROUP] = high[fro : fro + GROUP]
                    stacked[b, base + gap : base + gap + GROUP] = low[fro : fro + GROUP]
                    stacked[b, base + 2 * gap : base + 2 * gap + GROUP] = high[fro : fro + GROUP]
        for b in range(samples):
            result = jnp.dot(mist[...], stacked[b], preferred_element_type=f32)
            for piece in range(length // span):
                index = b * (length // span) + piece
                values = result[piece * span : (piece + 1) * span]
                misfit[n, index] = values
                parts[n, index] = values.astype(bf16)
        for k in range(1, groups):
            copy = remote(
                parts.at[n, group_at[k]], landed.at[k - 1, n], a_send.at[k - 1, n],
                a_recv.at[k - 1, n], (group_at[k], par),
            )
            copy.start()
            a_copies.append(copy)

    for copy in c_copies:
        copy.wait_recv()
    west_tile, east_tile, south_tile, north_tile = beside(par)
    west_rim, east_rim, south_rim, north_rim = (
        rims[index].astype(f32) for index in (west_tile, east_tile, south_tile, north_tile)
    )
    sums = around(
        own,
        chunks,
        lambda j: pltpu.roll(west_rim, LANES - chunks - j, 1),
        lambda j: pltpu.roll(east_rim, TSIDE - 1 - j, 1),
        jnp.where(lane < 16, pltpu.roll(south_rim, 48, 1), pltpu.roll(south_rim, 32, 1)),
        jnp.where(lane >= LANES - 16, pltpu.roll(north_rim, 64, 1), pltpu.roll(north_rim, 80, 1)),
    )
    for j in range(chunks):
        strength = coupling[:, j * LANES : (j + 1) * LANES]
        diagonal = kappa[:, j * LANES : (j + 1) * LANES] + 4.0 * strength
        at = slice(j * LANES % WIDE, j * LANES % WIDE + LANES)
        prior[j * LANES // WIDE, :, at] = diagonal * own[j] - strength * sums[j]

    def prepare(tile, carry):
        strength = couplings[tile]
        rate = 1.0 / (kappas[tile] + 4.0 * strength)
        start[tile] = jnp.broadcast_to(rate, (rows, cells))
        ratio[tile] = jnp.broadcast_to(strength * rate, (rows, cells))
        return carry

    lax.fori_loop(0, tiles, prepare, 0)
    even[tiles] = jnp.zeros((rows, cells), f32)
    odd[tiles] = jnp.zeros((rows, cells), f32)

    e_copies, b_copies = [], []
    for n in range(columns):
        total = misfit[n, sens] + prior[n]
        for k in range(1, groups):
            a_copies[n * (groups - 1) + k - 1].wait_recv()
            total = total + landed[k - 1, n].astype(f32)
        exact[n] = total.reshape(tiles, rows, WIDE)
        grad[n] = exact[n].astype(bf16)
        for q in range(1, tiles):
            copy = remote(
                exact.at[n, tile_at[q]], grad_in.at[par, n], b_send.at[n, q - 1],
                b_recv.at[n, q - 1], (sens, tile_at[q]),
            )
            copy.start()
            b_copies.append(copy)
        for k in range(1, groups):
            copy = remote(
                grad.at[n], grad_all.at[sens, n], e_send.at[n, k - 1], e_recv.at[n, k - 1],
                (group_at[k], par),
            )
            copy.start()
            e_copies.append(copy)
        grad_in[par, n] = exact[n, par]
        grad_all[sens, n] = grad[n]

    for copy in b_copies:
        copy.wait_recv()

    def begin(tile, carry):
        for n in range(columns):
            at = slice(n * WIDE, (n + 1) * WIDE)
            values = grad_in[tile, n] * start[tile, :, at]
            start[tile, :, at] = values
            even[tile, :, at] = values
        return carry

    lax.fori_loop(0, tiles, begin, 0)

    def relax(tile, old):
        west, east, south, north = beside(tile)

        def load(index, j):
            return old[index, :, j * LANES : (j + 1) * LANES]

        sums = around(
            [load(tile, j) for j in range(chunks)],
            chunks,
            lambda j: pltpu.roll(load(west, j), LANES - TSIDE + 1, 1),
            lambda j: pltpu.roll(load(east, j), TSIDE - 1, 1),
            pltpu.roll(load(south, chunks - 1), TSIDE, 1),
            pltpu.roll(load(north, 0), LANES - TSIDE, 1),
        )
        for j, total in enumerate(sums):
            at = slice(j * LANES, (j + 1) * LANES)
            yield at, start[tile, :, at] + ratio[tile, :, at] * total

    def sweep(count):
        old, new = (even, odd) if count % 2 == 0 else (odd, even)

        def one(tile, carry):
            for at, values in relax(tile, old):
                new[tile, :, at] = values
            return carry

        lax.fori_loop(0, tiles, one, 0, unroll=2)

    for count in range(SWEEPS - 2):
        sweep(count)
    last = even if SWEEPS % 2 == 0 else odd
    d_copies = []
    for q in list(range(1, tiles)) + [0]:
        for at, values in relax(tile_at[q], last):
            dir_send[tile_at[q], :, at] = values.astype(bf16)
        if q:
            copy = remote(
                dir_send.at[tile_at[q]], dir_all.at[sens, par], d_send.at[q - 1], d_recv.at[q - 1],
                (sens, tile_at[q]),
            )
            copy.start()
            d_copies.append(copy)
    dir_all[sens, par] = dir_send[par]
    f_copies = []
    for q in range(tiles):
        if q:
            d_copies[q - 1].wait_recv()
        piece = dir_all.at[sens, source_at[q]]
        for k in range(1, groups):
            copy = remote(
                piece, piece, f_send.at[k - 1, q], f_recv.at[k - 1, q], (group_at[k], par)
            )
            copy.start()
            f_copies.append(copy)

    def place_at(index, j):
        first = index * rows
        sample, time = first // length, lax.rem(first, length)
        return pl.ds(time * stride + samples * j + sample, rows, stride=stride)

    for copy in e_copies:
        copy.wait_recv()

    def unpack_grad(index, carry):
        group, block = index // tiles, lax.rem(index, tiles)
        for j in range(chunks):
            at = slice(j * LANES % WIDE, j * LANES % WIDE + LANES)
            grad_out[place_at(index, j), :] = grad_all[
                group, j * LANES // WIDE, block, :, at
            ].astype(f32)
        return carry

    lax.fori_loop(0, groups * tiles, unpack_grad, 0)
    for copy in f_copies:
        copy.wait_recv()

    def unpack_dir(index, carry):
        group, block = index // tiles, lax.rem(index, tiles)
        for j in range(chunks):
            at = slice(j * LANES, (j + 1) * LANES)
            dir_out[place_at(index, j), :] = dir_all[group, block, :, at].astype(f32)
        return carry

    lax.fori_loop(0, groups * tiles, unpack_dir, 0)
    for copy in p_copies + c_copies + a_copies + e_copies + b_copies + d_copies + f_copies:
        copy.wait_send()


def per_device(
    kernel, param, observed, noise_scale, robust_flags, kappa_field, coupling, neighbours
):
    length, samples, cells = param.shape
    parts, count, sensors = kernel.shape[:3]
    groups, tiles = lax.axis_size("sens"), lax.axis_size("par")
    chunks, columns = cells // LANES, cells // WIDE
    freqs = -(-count // GROUP)
    span = length * samples // groups
    rows = span // tiles
    block = (rows, cells)
    raw = param.reshape(length, samples, chunks, LANES).transpose(0, 2, 1, 3)
    raw = raw.reshape(length * chunks * samples, LANES)
    consts = all_tables(length)
    vmem, smem = pl.BlockSpec(memory_space=pltpu.VMEM), pl.BlockSpec(memory_space=pltpu.SMEM)
    dma, scratch = pltpu.SemaphoreType.DMA, pltpu.VMEM
    out = jax.ShapeDtypeStruct(raw.shape, f32)
    sems = [
        (freqs, tiles - 1), (tiles - 1,), (2, tiles - 1), (groups - 1, columns),
        (columns, groups - 1), (columns, tiles - 1), (tiles - 1,), (groups - 1, tiles),
    ]
    gradient, direction = pl.pallas_call(
        functools.partial(main_kernel, groups, tiles),
        out_shape=(out, out),
        in_specs=[pl.BlockSpec(memory_space=pl.ANY)] + [vmem] * 6 + [smem] + [vmem] * 4,
        out_specs=(vmem, vmem),
        scratch_shapes=[
            scratch((freqs, parts, GROUP * sensors, cells), bf16),
            scratch((samples, 2 * length, cells), bf16),
            scratch((freqs, 2 * samples * GROUP, cells), bf16),
            scratch((freqs, HALF, LANES), f32),
            scratch((length, LANES), f32),
            scratch((length, LANES), f32),
            scratch((freqs, 2 * samples * GROUP, 2 * WIDE), bf16),
            scratch((samples, 3 * freqs * 2 * GROUP, WIDE), bf16),
            scratch((columns, groups, span, WIDE), f32),
            scratch((columns, groups, span, WIDE), bf16),
            scratch((groups - 1, columns, span, WIDE), bf16),
            scratch((columns, span, WIDE), f32),
            scratch((span, LANES), bf16),
            scratch((tiles + 1, span, LANES), bf16),
            scratch((tiles, 1, cells), f32),
            scratch((tiles, 1, cells), f32),
            scratch((columns, tiles, rows, WIDE), bf16),
            scratch((columns, tiles, rows, WIDE), f32),
            scratch((tiles, columns, rows, WIDE), f32),
            scratch((tiles,) + block, f32),
            scratch((tiles,) + block, f32),
            scratch((tiles + 1,) + block, f32),
            scratch((tiles + 1,) + block, f32),
            scratch((tiles,) + block, bf16),
            scratch((groups, columns, tiles, rows, WIDE), bf16),
            scratch((groups, tiles) + block, bf16),
            scratch((tiles - 1, freqs, HALF, LANES), f32),
            dma((freqs, parts)),
        ]
        + [dma(shape) for shape in sems for _ in range(2)],
        compiler_params=pltpu.CompilerParams(collective_id=0, has_side_effects=True),
    )(
        kernel.reshape(parts, count * sensors, cells), raw, observed, noise_scale[None],
        robust_flags, kappa_field[None], coupling[None], neighbours.T, *consts,
    )

    def restore(values):
        values = values.reshape(length, chunks, samples, LANES).transpose(0, 2, 1, 3)
        return values.reshape(param.shape)

    return restore(gradient), restore(direction)


def solution(mesh):
    return jax.shard_map(
        per_device,
        mesh=mesh,
        in_specs=(
            P(None, None, "sens", "par"),
            P(None, None, "par"),
            P("sens", None),
            P("sens"),
            P("sens", None),
            P("par"),
            P("par"),
            P(),
        ),
        out_specs=(P(None, None, "par"), P(None, None, "par")),
        check_vma=False,
    )
```

profile of v0, /device:TPU:0, one launch (start us, length us, event | category | flops | bytes accessed | tf_op | source)
XLA Modules:
  0.0 56.7 jit_solution(7139226920193401521)
XLA Ops:
  0.6 51.5 %shard_map.131 = (f32[2048,128]{1,0:T(8,128)}, f32[2048,128]{1,0:T(8,128)}) custom-call(bf16[2,2064,1024]{2,1,0:T(8,128)(2,1)} %bitcast.20, f32[2048,128]{1,0:T(8,128)} %bitcast.23, f32[16,128]{1,0:T(8,128)} %observed.1, f32[1,16]{1,0:T(1,128)} %bitcast.27, s32[16,128]{1,0:T(8,128)} %flags.1, f32[1,1024]{1,0:T(1,128)} %bitcast.24, f32[1,1024]{1,0:T(1,128)} %bitcast.25, ...), custom_call_target="tpu_custom_call" | custom-call | tf_op jit(solution)/shard_map/pallas_call | solution.py:520
  52.1 2.3 %copy.19 = f32[128,2,1024]{2,1,0:T(2,128)} copy(f32[128,2,1024]{2,1,0:T(2,128)} %bitcast.22) | data formatting | bytes 2097152
  54.4 2.3 %copy.20 = f32[128,2,1024]{2,1,0:T(2,128)} copy(f32[128,2,1024]{2,1,0:T(2,128)} %bitcast.21) | data formatting | bytes 2097152
where the time goes:
time: 56.9 us; the launch traced here: 56.7 us
  Pallas kernels  51.5 us (91%)
  local copies, waits for them, and re-layouts  4.52 us (8%)
  between operations  0.64 us (1%)
    pallas_call x1, Pallas kernels, per_device(): pl.pallas_call(functools.partial(main_kernel, groups, tiles), out_shape=(...  51.5 us
    unnamed x2, local copies, waits for them, and re-layouts  4.52 us

commit v1 on v0

--- a/solution.py
+++ b/solution.py
@@ -103,12 +103,12 @@
 
 def main_kernel(
     groups, tiles,
-    kernel, param, observed, noise, flags, kappa, coupling, near, fore, trans, back, mist,
-    grad_out, dir_out,
-    blocks, halved, spectrum, packed, seen, bounded, wide, stacked, misfit, parts, landed, prior,
-    rim, rims, kappas, couplings, grad, exact, grad_in, start, ratio, even, odd, dir_send, grad_all, dir_all,
-    predicted, k_sem, k_send, k_recv, r_send, r_recv, c_send, c_recv, a_send, a_recv, e_send, e_recv,
-    b_send, b_recv, d_send, d_recv, f_send, f_recv,
+    kernel, param_in, fore_in, trans_in, back_in, mist_in, observed, noise, flags, kappa, coupling, near,
+    grad_all, dir_all,
+    param, fore, trans, back, mist, blocks, halved, spectrum, packed, seen, bounded, wide, stacked,
+    misfit, parts, landed, prior, rim, rims, kappas, couplings, grad, exact, grad_in, start, ratio,
+    even, odd, dir_send, mine_out, others, k_sem, l_sem, k_send, k_recv, r_send, r_recv, c_send, c_recv,
+    a_send, a_recv, e_send, e_recv, b_send, b_recv, d_send, d_recv, f_send, f_recv,
 ):
     sens, par = lax.axis_index("sens"), lax.axis_index("par")
     sensors, length = observed.shape
@@ -131,18 +131,43 @@
     for q in range(1, tiles):
         pl.semaphore_signal(barrier, inc=1, device_id=(sens, tile_at[q]), device_id_type=MESH)
 
-    loads = []
-    for g in range(freqs):
-        size = GROUP * sensors if g < full else (length + 1 - full * GROUP) * sensors
+    early = [
+        pltpu.make_async_copy(source, target, l_sem.at[index])
+        for index, (source, target) in enumerate(
+            [(param_in, param), (fore_in, fore), (trans_in, trans), (back_in, back), (mist_in, mist)]
+        )
+    ]
+
+    def fetch(g, i, size):
+        return pltpu.make_async_copy(
+            kernel.at[i, pl.ds(g * GROUP * sensors, size)],
+            blocks.at[g, i, pl.ds(0, size)],
+            k_sem.at[g, i],
+        )
+
+    whole, rest = GROUP * sensors, (length + 1 - full * GROUP) * sensors
+    for copy in early[:2]:
+        copy.start()
+
+    def begin_fetch(g, carry):
         for i in range(pieces):
-            copy = pltpu.make_async_copy(
-                kernel.at[i, pl.ds(g * GROUP * sensors, size)],
-                blocks.at[g, i, pl.ds(0, size)],
-                k_sem.at[g, i],
-            )
-            copy.start()
-            loads.append(copy)
-
+            fetch(g, i, whole).start()
+        return carry
+
+    lax.fori_loop(0, full, begin_fetch, 0)
+    for i in range(pieces):
+        fetch(full, i, rest).start()
+    for copy in early[2:]:
+        copy.start()
+
+    copies = LANES // sensors
+    seen[...] = jnp.concatenate([observed[...]] * copies, 0).T
+    bounded[...] = jnp.concatenate([flags[...].astype(f32)] * copies, 0).T
+    deviation = jnp.concatenate([noise[...]] * copies, 1)
+    inverse = 1.0 / deviation
+
+    for copy in early[:2]:
+        copy.wait()
     for b in range(samples):
         for j in range(chunks):
             high, low = split(param[pl.ds(samples * j + b, length, stride=stride), :])
@@ -161,12 +186,6 @@
                     to, fro = (k * samples + b) * GROUP, (g * 2 + k) * GROUP
                     spectrum[g, to : to + GROUP, at] = rounded[fro : fro + GROUP]
 
-    copies = LANES // sensors
-    seen[...] = jnp.concatenate([observed[...]] * copies, 0).T
-    bounded[...] = jnp.concatenate([flags[...].astype(f32)] * copies, 0).T
-    deviation = jnp.concatenate([noise[...]] * copies, 1)
-    inverse = 1.0 / deviation
-
     lanes64 = lax.broadcasted_iota(jnp.int32, (2 * samples * GROUP, WIDE), 1) // sensors
     rows64 = lax.rem(lax.broadcasted_iota(jnp.int32, (2 * samples * GROUP, WIDE), 0), GROUP)
     keep = lanes64 == rows64
@@ -182,34 +201,60 @@
             out = jnp.where(place == r, total[r * HALF : (r + 1) * HALF], out)
         return out
 
-    p_copies = []
     for g in range(freqs):
+        size = whole if g < full else rest
         for i in range(pieces):
-            loads[g * pieces + i].wait()
+            fetch(g, i, size).wait()
         folded = []
         for i in range(pieces):
+            product = lax.dot_general(
+                spectrum[g], blocks[g, i, :size], LAST, preferred_element_type=f32
+            )
             if g < full:
-                product = lax.dot_general(
-                    spectrum[g], blocks[g, i], LAST, preferred_element_type=f32
-                )
                 product = jnp.where(keep, product, 0.0)
                 folded.append(product[:, :LANES] + product[:, LANES:])
             else:
-                product = lax.dot_general(
-                    spectrum[g], blocks[g, i, :sensors], LAST, preferred_element_type=f32
-                )
                 filler = jnp.zeros((product.shape[0], LANES - sensors), f32)
                 folded.append(jnp.concatenate([product, filler], 1))
         packed[g] = pack(*folded)
-        if g == 0:
-            pl.semaphore_wait(barrier, groups + tiles - 2)
-        for q in range(1, tiles):
-            copy = remote(
-                packed.at[g], predicted.at[q - 1, g], k_send.at[g, q - 1], k_recv.at[g, q - 1],
-                (sens, tile_at[q]),
-            )
-            copy.start()
-            p_copies.append(copy)
+
+    for copy in early[2:]:
+        copy.wait()
+    high, low = split_wide(packed[...].reshape(freqs * HALF, LANES))
+    right = jnp.concatenate([high, low], 0).astype(bf16)
+    both = jnp.dot(trans[...], right, preferred_element_type=f32)
+    both = both[: 4 * length] + both[4 * length :]
+
+    def lane_group(count):
+        where = lax.broadcasted_iota(jnp.int32, (count, LANES), 1) // sensors
+        kind = where // (2 * samples) * 2 + lax.rem(where, 2)
+        return lax.rem(where // 2, samples), kind
+
+    kind = lane_group(length)[1]
+    series = both[:length]
+    for part in range(1, 4):
+        series = jnp.where(kind == part, both[part * length : (part + 1) * length], series)
+    series = series + jnp.where(
+        lax.rem(kind, 2) == 0, pltpu.roll(series, LANES - sensors, 1), pltpu.roll(series, sensors, 1)
+    )
+    series = series + pltpu.roll(series, LANES // 2, 1)
+    short = length // 4
+    sample_of, kind = lane_group(short)
+    share = series[:short]
+    for part in range(1, 4):
+        share = jnp.where(kind == part, series[part * short : (part + 1) * short], share)
+    mine_out[...] = share
+
+    near_first = sorted(range(tiles), key=lambda q: min(q, tiles - q))
+    far_first = near_first[:0:-1]
+    pl.semaphore_wait(barrier, groups + tiles - 2)
+    p_copies = []
+    for q in far_first:
+        copy = remote(
+            mine_out, others.at[q - 1], k_send.at[q - 1], k_recv.at[q - 1], (sens, tile_at[q])
+        )
+        copy.start()
+        p_copies.append(copy)
 
     first = sens * span
     own_sample, own_time = first // length, lax.rem(first, length)
@@ -252,21 +297,14 @@
 
     for copy in p_copies:
         copy.wait_recv()
-    total = packed[...]
+    total = mine_out[...]
     for q in range(tiles - 1):
-        total = total + predicted[q]
-    high, low = split_wide(total.reshape(freqs * HALF, LANES))
-    right = jnp.concatenate([high, low], 0).astype(bf16)
-    both = jnp.dot(trans[...], right, preferred_element_type=f32)
-    both = both[: 4 * length] + both[4 * length :]
-    where = lax.broadcasted_iota(jnp.int32, (length, LANES), 1) // sensors
-    sample_of, kind = lax.rem(where // 2, samples), where // (2 * samples) * 2 + lax.rem(where, 2)
-    series = both[:length]
-    for part in range(1, 4):
-        series = jnp.where(kind == part, both[part * length : (part + 1) * length], series)
+        total = total + others[q]
     adjoint = []
     for b in range(samples):
-        mine = jnp.where(sample_of == b, series, 0.0)
+        mine = jnp.concatenate(
+            [jnp.where((sample_of == b) & (kind == part), total, 0.0) for part in range(4)], 0
+        )
         for step in range(copies.bit_length() - 1):
             mine = mine + pltpu.roll(mine, sensors << step, 1)
         scaled = (mine - seen[...]) * inverse
@@ -387,13 +425,13 @@
             b_copies.append(copy)
         for k in range(1, groups):
             copy = remote(
-                grad.at[n], grad_all.at[sens, n], e_send.at[n, k - 1], e_recv.at[n, k - 1],
+                grad.at[n], grad_all.at[n, sens], e_send.at[n, k - 1], e_recv.at[n, k - 1],
                 (group_at[k], par),
             )
             copy.start()
             e_copies.append(copy)
         grad_in[par, n] = exact[n, par]
-        grad_all[sens, n] = grad[n]
+        grad_all[n, sens] = grad[n]
 
     for copy in b_copies:
         copy.wait_recv()
@@ -434,13 +472,13 @@
                 new[tile, :, at] = values
             return carry
 
-        lax.fori_loop(0, tiles, one, 0, unroll=2)
+        lax.fori_loop(0, tiles, one, 0, unroll=min(tiles, 8))
 
     for count in range(SWEEPS - 2):
         sweep(count)
     last = even if SWEEPS % 2 == 0 else odd
-    d_copies = []
-    for q in list(range(1, tiles)) + [0]:
+    d_copies = {}
+    for q in far_first + [0]:
         for at, values in relax(tile_at[q], last):
             dir_send[tile_at[q], :, at] = values.astype(bf16)
         if q:
@@ -449,51 +487,67 @@
                 (sens, tile_at[q]),
             )
             copy.start()
-            d_copies.append(copy)
+            d_copies[q] = copy
     dir_all[sens, par] = dir_send[par]
     f_copies = []
-    for q in range(tiles):
-        if q:
-            d_copies[q - 1].wait_recv()
-        piece = dir_all.at[sens, source_at[q]]
-        for k in range(1, groups):
-            copy = remote(
-                piece, piece, f_send.at[k - 1, q], f_recv.at[k - 1, q], (group_at[k], par)
-            )
+
+    def onward(q, group, targets):
+        piece = dir_all.at[group, source_at[q]]
+        out = []
+        for k, target in targets:
+            copy = remote(piece, piece, f_send.at[k, q], f_recv.at[k, q], (target, par))
             copy.start()
-            f_copies.append(copy)
-
-    def place_at(index, j):
-        first = index * rows
-        sample, time = first // length, lax.rem(first, length)
-        return pl.ds(time * stride + samples * j + sample, rows, stride=stride)
-
+            out.append(copy)
+        f_copies.extend(out)
+        return out
+
+    if groups == 4:
+        beside_x, beside_y = sens + 1 - 2 * lax.rem(sens, 2), lax.rem(sens + 2, groups)
+        direct, passed = {}, []
+
+        def relay(index):
+            q = near_first[index]
+            origin, target = (beside_x, beside_y) if index % 2 == 0 else (beside_y, beside_x)
+            direct[q][index % 2].wait_recv()
+            passed.extend(onward(q, origin, [(2, target)]))
+
+        lag = 2
+        for index, q in enumerate(near_first):
+            if q:
+                d_copies[q].wait_recv()
+            direct[q] = onward(q, sens, [(0, beside_x), (1, beside_y)])
+            if index >= lag:
+                relay(index - lag)
+        for index in range(tiles - lag, tiles):
+            relay(index)
+        for index, q in enumerate(near_first):
+            direct[q][1 - index % 2].wait_recv()
+        for copy in passed:
+            copy.wait_recv()
+    else:
+        for q in near_first:
+            if q:
+                d_copies[q].wait_recv()
+            onward(q, sens, [(k - 1, group_at[k]) for k in range(1, groups)])
+        for copy in f_copies:
+            copy.wait_recv()
     for copy in e_copies:
         copy.wait_recv()
-
-    def unpack_grad(index, carry):
-        group, block = index // tiles, lax.rem(index, tiles)
-        for j in range(chunks):
-            at = slice(j * LANES % WIDE, j * LANES % WIDE + LANES)
-            grad_out[place_at(index, j), :] = grad_all[
-                group, j * LANES // WIDE, block, :, at
-            ].astype(f32)
-        return carry
-
-    lax.fori_loop(0, groups * tiles, unpack_grad, 0)
-    for copy in f_copies:
-        copy.wait_recv()
-
-    def unpack_dir(index, carry):
-        group, block = index // tiles, lax.rem(index, tiles)
-        for j in range(chunks):
-            at = slice(j * LANES, (j + 1) * LANES)
-            dir_out[place_at(index, j), :] = dir_all[group, block, :, at].astype(f32)
-        return carry
-
-    lax.fori_loop(0, groups * tiles, unpack_dir, 0)
+    d_copies = list(d_copies.values())
     for copy in p_copies + c_copies + a_copies + e_copies + b_copies + d_copies + f_copies:
         copy.wait_send()
+
+
+def finish_kernel(stride, grad, direction, grad_out, dir_out):
+    samples, count, rows, cells = direction.shape
+    for b in range(samples):
+        for i in range(count):
+            for j in range(cells // LANES):
+                to = pl.ds(i * rows * stride + samples * j + b, rows, stride=stride)
+                at = slice(j * LANES, (j + 1) * LANES)
+                n, inner = j * LANES // WIDE, slice(j * LANES % WIDE, j * LANES % WIDE + LANES)
+                grad_out[to, :] = grad[n, b, i, :, inner].astype(f32)
+                dir_out[to, :] = direction[b, i, :, at].astype(f32)
 
 
 def per_device(
@@ -512,17 +566,22 @@
     consts = all_tables(length)
     vmem, smem = pl.BlockSpec(memory_space=pltpu.VMEM), pl.BlockSpec(memory_space=pltpu.SMEM)
     dma, scratch = pltpu.SemaphoreType.DMA, pltpu.VMEM
-    out = jax.ShapeDtypeStruct(raw.shape, f32)
+    hbm = pl.BlockSpec(memory_space=pl.ANY)
     sems = [
-        (freqs, tiles - 1), (tiles - 1,), (2, tiles - 1), (groups - 1, columns),
+        (tiles - 1,), (tiles - 1,), (2, tiles - 1), (groups - 1, columns),
         (columns, groups - 1), (columns, tiles - 1), (tiles - 1,), (groups - 1, tiles),
     ]
-    gradient, direction = pl.pallas_call(
+    grad_all, dir_all = pl.pallas_call(
         functools.partial(main_kernel, groups, tiles),
-        out_shape=(out, out),
-        in_specs=[pl.BlockSpec(memory_space=pl.ANY)] + [vmem] * 6 + [smem] + [vmem] * 4,
+        out_shape=(
+            jax.ShapeDtypeStruct((columns, groups, tiles, rows, WIDE), bf16),
+            jax.ShapeDtypeStruct((groups, tiles) + block, bf16),
+        ),
+        in_specs=[hbm] * 6 + [vmem] * 5 + [smem],
         out_specs=(vmem, vmem),
-        scratch_shapes=[
+        scratch_shapes=[scratch(raw.shape, f32)]
+        + [scratch(table.shape, bf16) for table in consts]
+        + [
             scratch((freqs, parts, GROUP * sensors, cells), bf16),
             scratch((samples, 2 * length, cells), bf16),
             scratch((freqs, 2 * samples * GROUP, cells), bf16),
@@ -547,16 +606,34 @@
             scratch((tiles + 1,) + block, f32),
             scratch((tiles + 1,) + block, f32),
             scratch((tiles,) + block, bf16),
-            scratch((groups, columns, tiles, rows, WIDE), bf16),
-            scratch((groups, tiles) + block, bf16),
-            scratch((tiles - 1, freqs, HALF, LANES), f32),
+            scratch((length // 4, LANES), f32),
+            scratch((tiles - 1, length // 4, LANES), f32),
             dma((freqs, parts)),
+            dma((5,)),
         ]
         + [dma(shape) for shape in sems for _ in range(2)],
         compiler_params=pltpu.CompilerParams(collective_id=0, has_side_effects=True),
     )(
-        kernel.reshape(parts, count * sensors, cells), raw, observed, noise_scale[None],
-        robust_flags, kappa_field[None], coupling[None], neighbours.T, *consts,
+        kernel.reshape(parts, count * sensors, cells), raw, *consts, observed, noise_scale[None],
+        robust_flags, kappa_field[None], coupling[None], neighbours.T,
+    )
+
+    steps = max(1, length // rows // 2)
+    each = length // rows // steps
+    out = jax.ShapeDtypeStruct(raw.shape, f32)
+    out_spec = pl.BlockSpec((raw.shape[0] // steps, LANES), lambda s: (s, 0))
+    gradient, direction = pl.pallas_call(
+        functools.partial(finish_kernel, chunks * samples),
+        out_shape=(out, out),
+        grid=(steps,),
+        in_specs=[
+            pl.BlockSpec((columns, samples, each, rows, WIDE), lambda s: (0, 0, s, 0, 0)),
+            pl.BlockSpec((samples, each) + block, lambda s: (0, s, 0, 0)),
+        ],
+        out_specs=(out_spec, out_spec),
+    )(
+        grad_all.reshape(columns, samples, length // rows, rows, WIDE),
+        dir_all.reshape((samples, length // rows) + block),
     )
 
     def restore(values):

time: 56.9 us -> 61 us (1.072)
  Pallas kernels: 51.5 us -> 59.9 us
  local copies, waits for them, and re-layouts: 4.52 us -> 0 us
    pallas_call x0 -> x1, Pallas kernels: none -> 5.51 us  [per_device(): pl.pallas_call(functools.partial(finish_kernel, chunks * samples), out_sh...]
    unnamed x2 -> x0, local copies, waits for them, and re-layouts: 4.52 us -> none
    pallas_call x1, Pallas kernels: 51.5 us -> 54.4 us  [per_device(): pl.pallas_call(functools.partial(main_kernel, groups, tiles), out_shape=(...]
where the time goes in v1:
time: 61 us; the launch traced here: 60.6 us
  Pallas kernels  59.9 us (98%)
  between operations  0.64 us (1%)
    pallas_call x1, Pallas kernels, per_device(): pl.pallas_call(functools.partial(main_kernel, groups, tiles), out_shape=(...  54.4 us
    pallas_call x1, Pallas kernels, per_device(): pl.pallas_call(functools.partial(finish_kernel, chunks * samples), out_sh...  5.51 us

profile of v1, /device:TPU:0, one launch (start us, length us, event | category | flops | bytes accessed | tf_op | source)
XLA Modules:
  0.0 60.6 jit_solution(2392985379529078773)
XLA Ops:
  0.6 54.4 %shard_map.131 = (bf16[4,4,8,8,256]{4,3,2,1,0:T(8,128)(2,1)}, bf16[4,8,8,1024]{3,2,1,0:T(8,128)(2,1)}) custom-call(bf16[2,2064,1024]{2,1,0:T(8,128)(2,1)} %bitcast.22, f32[2048,128]{1,0:T(8,128)} %bitcast.23, bf16[576,256]{1,0:T(8,128)(2,1)} %constant.8.clone.fore_in, bf16[1024,144]{1,0:T(8,128)(2,1)} %constant.9.clone.trans_in, ...), custom_call_target="tpu_custom_call" | custom-call | tf_op jit(solution)/shard_map/pallas_call | solution.py:574
  55.0 5.5 %shard_map.132 = (f32[2048,128]{1,0:T(8,128)}, f32[2048,128]{1,0:T(8,128)}) custom-call(bf16[4,2,16,8,256]{4,3,2,1,0:T(8,128)(2,1)} %bitcast.24, bf16[2,16,8,1024]{3,2,1,0:T(8,128)(2,1)} %bitcast.25), custom_call_target="tpu_custom_call" | custom-call | tf_op jit(solution)/shard_map/pallas_call | solution.py:625

commit v2 on v1

--- a/solution.py
+++ b/solution.py
@@ -66,7 +66,11 @@
     misfit = np.concatenate(
         [high[:, main], high[:, main], low[:, main], high[:, rest], high[:, rest], low[:, rest]], 1
     )
-    return pairs(fore), pairs(trans), pairs(back), misfit
+
+    def fill(table):
+        return np.pad(table, ((0, 0), (0, -table.shape[1] % LANES)))
+
+    return tuple(fill(table) for table in (pairs(fore), pairs(trans), pairs(back), misfit))
 
 
 def split(values):
@@ -222,7 +226,7 @@
         copy.wait()
     high, low = split_wide(packed[...].reshape(freqs * HALF, LANES))
     right = jnp.concatenate([high, low], 0).astype(bf16)
-    both = jnp.dot(trans[...], right, preferred_element_type=f32)
+    both = jnp.dot(trans[:, : right.shape[0]], right, preferred_element_type=f32)
     both = both[: 4 * length] + both[4 * length :]
 
     def lane_group(count):
@@ -245,11 +249,10 @@
         share = jnp.where(kind == part, series[part * short : (part + 1) * short], share)
     mine_out[...] = share
 
-    near_first = sorted(range(tiles), key=lambda q: min(q, tiles - q))
-    far_first = near_first[:0:-1]
+    others_at = list(range(1, tiles))
     pl.semaphore_wait(barrier, groups + tiles - 2)
     p_copies = []
-    for q in far_first:
+    for q in others_at:
         copy = remote(
             mine_out, others.at[q - 1], k_send.at[q - 1], k_recv.at[q - 1], (sens, tile_at[q])
         )
@@ -363,7 +366,7 @@
                     stacked[b, base + gap : base + gap + GROUP] = low[fro : fro + GROUP]
                     stacked[b, base + 2 * gap : base + 2 * gap + GROUP] = high[fro : fro + GROUP]
         for b in range(samples):
-            result = jnp.dot(mist[...], stacked[b], preferred_element_type=f32)
+            result = jnp.dot(mist[:, : stacked.shape[1]], stacked[b], preferred_element_type=f32)
             for piece in range(length // span):
                 index = b * (length // span) + piece
                 values = result[piece * span : (piece + 1) * span]
@@ -478,7 +481,7 @@
         sweep(count)
     last = even if SWEEPS % 2 == 0 else odd
     d_copies = {}
-    for q in far_first + [0]:
+    for q in others_at + [0]:
         for at, values in relax(tile_at[q], last):
             dir_send[tile_at[q], :, at] = values.astype(bf16)
         if q:
@@ -491,46 +494,18 @@
     dir_all[sens, par] = dir_send[par]
     f_copies = []
 
-    def onward(q, group, targets):
-        piece = dir_all.at[group, source_at[q]]
-        out = []
-        for k, target in targets:
-            copy = remote(piece, piece, f_send.at[k, q], f_recv.at[k, q], (target, par))
+    for q in range(tiles):
+        if q:
+            d_copies[q].wait_recv()
+        piece = dir_all.at[sens, source_at[q]]
+        for k in range(1, groups):
+            copy = remote(
+                piece, piece, f_send.at[k - 1, q], f_recv.at[k - 1, q], (group_at[k], par)
+            )
             copy.start()
-            out.append(copy)
-        f_copies.extend(out)
-        return out
-
-    if groups == 4:
-        beside_x, beside_y = sens + 1 - 2 * lax.rem(sens, 2), lax.rem(sens + 2, groups)
-        direct, passed = {}, []
-
-        def relay(index):
-            q = near_first[index]
-            origin, target = (beside_x, beside_y) if index % 2 == 0 else (beside_y, beside_x)
-            direct[q][index % 2].wait_recv()
-            passed.extend(onward(q, origin, [(2, target)]))
-
-        lag = 2
-        for index, q in enumerate(near_first):
-            if q:
-                d_copies[q].wait_recv()
-            direct[q] = onward(q, sens, [(0, beside_x), (1, beside_y)])
-            if index >= lag:
-                relay(index - lag)
-        for index in range(tiles - lag, tiles):
-            relay(index)
-        for index, q in enumerate(near_first):
-            direct[q][1 - index % 2].wait_recv()
-        for copy in passed:
-            copy.wait_recv()
-    else:
-        for q in near_first:
-            if q:
-                d_copies[q].wait_recv()
-            onward(q, sens, [(k - 1, group_at[k]) for k in range(1, groups)])
-        for copy in f_copies:
-            copy.wait_recv()
+            f_copies.append(copy)
+    for copy in f_copies:
+        copy.wait_recv()
     for copy in e_copies:
         copy.wait_recv()
     d_copies = list(d_copies.values())
@@ -618,7 +593,7 @@
         robust_flags, kappa_field[None], coupling[None], neighbours.T,
     )
 
-    steps = max(1, length // rows // 2)
+    steps = 2
     each = length // rows // steps
     out = jax.ShapeDtypeStruct(raw.shape, f32)
     out_spec = pl.BlockSpec((raw.shape[0] // steps, LANES), lambda s: (s, 0))

time: 61 us -> 52.2 us (0.86)
  Pallas kernels: 59.9 us -> 51.3 us
    pallas_call x1, Pallas kernels: 54.4 us -> 48.7 us  [per_device(): pl.pallas_call(functools.partial(main_kernel, groups, tiles), out_shape=(...]
    pallas_call x1, Pallas kernels: 5.51 us -> 2.67 us  [per_device(): pl.pallas_call(functools.partial(finish_kernel, chunks * samples), out_sh...]
where the time goes in v2:
time: 52.2 us; the launch traced here: 52 us
  Pallas kernels  51.3 us (98%)
  between operations  0.64 us (1%)
    pallas_call x1, Pallas kernels, per_device(): pl.pallas_call(functools.partial(main_kernel, groups, tiles), out_shape=(...  48.7 us
    pallas_call x1, Pallas kernels, per_device(): pl.pallas_call(functools.partial(finish_kernel, chunks * samples), out_sh...  2.67 us

profile of v2, /device:TPU:0, one launch (start us, length us, event | category | flops | bytes accessed | tf_op | source)
XLA Modules:
  0.0 52.0 jit_solution(1578995170161639720)
XLA Ops:
  0.6 48.7 %shard_map.131 = (bf16[4,4,8,8,256]{4,3,2,1,0:T(8,128)(2,1)}, bf16[4,8,8,1024]{3,2,1,0:T(8,128)(2,1)}) custom-call(bf16[2,2064,1024]{2,1,0:T(8,128)(2,1)} %bitcast.22, f32[2048,128]{1,0:T(8,128)} %bitcast.23, bf16[576,256]{1,0:T(8,128)(2,1)} %constant.8.clone.fore_in, bf16[1024,256]{1,0:T(8,128)(2,1)} %constant.9.clone.trans_in, ...), custom_call_target="tpu_custom_call" | custom-call | tf_op jit(solution)/shard_map/pallas_call | solution.py:549
  49.3 2.7 %shard_map.132 = (f32[2048,128]{1,0:T(8,128)}, f32[2048,128]{1,0:T(8,128)}) custom-call(bf16[4,2,16,8,256]{4,3,2,1,0:T(8,128)(2,1)} %bitcast.24, bf16[2,16,8,1024]{3,2,1,0:T(8,128)(2,1)} %bitcast.25), custom_call_target="tpu_custom_call" | custom-call | tf_op jit(solution)/shard_map/pallas_call | solution.py:600
